TPU v7x, 32 devices: a whole 2x2x4 slice. The times are simulated.
32 devices in a mesh: groups: 2 (over x), ctx: 16 (over z, y, core).
Axes of the slice: x: 2, y: 2, z: 4, core: 2. Of those that a mesh axis runs over, the one named last changes fastest.
Arguments:
- query_input: bfloat16 [32, 1536], P('groups'), parts along dimension 0, may hold values from -20 to 20
- query_gain: bfloat16 [1536], replicated, may hold values from 0.5 to 1.5
- nope_weight: bfloat16 [1536, 4096], P(None, 'ctx'), may hold values from -0.15625 to 0.15625
- rope_weight: bfloat16 [1536, 2048], P(None, 'ctx'), may hold values from -0.15625 to 0.15625
- key_up: bfloat16 [32, 128, 512], P('ctx'), may hold values from -0.5 to 0.5
- value_up: bfloat16 [32, 512, 128], P('ctx'), may hold values from -1 to 1
- out_weight: bfloat16 [4096, 7168], P('ctx'), may hold values from -0.09375 to 0.09375
- cache_latent: bfloat16 [4, 32768, 512], P('groups', 'ctx'), parts along dimension 0, may hold values from -8 to 8
- cache_rope: bfloat16 [4, 64, 32768], P('groups', None, 'ctx'), parts along dimension 0, may hold values from -256 to 256
- cached_length: int32 [4], P('groups'), parts along dimension 0, may hold values from 16384 to 32760, as said below
Outputs:
- attn_out: bfloat16 [32, 7168], P('groups'), parts along dimension 0
There are 2 independent parts, one for each index of `groups`. A program takes and returns all parts, laid end to end along the dimension named above; an argument that names none is the same for every part. Nothing has to cross between parts.
Inputs may be any that keep to these rules, and one draw needn't show every extreme that they name: `cached_length`: in every part one request has exactly 32760, so that its last new token sees the cache's last position.
All inputs are finite; a program needn't handle non-finite values.
Results may differ from a plain program's by a relative error of at most 0.012.
Values may be sent and summed in bfloat16 or wider, within the bound.
A program may use at most 128 MiB of HBM per device.

v0:
```python
import math
import jax
import jax.numpy as jnp
from jax import lax
from jax.sharding import PartitionSpec as P

mscale_yarn = 1.0 + 0.1 * math.log(40.0)
masked_score = -1e30


def attend_heads(
    latent_query, rope_query, cache_latent, cache_rope, cached_length, positions, softmax_scale
):
    row_count, head_count, latent_width = latent_query.shape
    rope_width = rope_query.shape[2]
    requests = cache_latent.shape[0]
    stretch_rows = row_count // requests
    peak_list, sum_list, pool_list = ([], [], [])
    for request in range(requests):
        flat_latent = latent_query[request * stretch_rows : (request + 1) * stretch_rows].reshape(
            stretch_rows * head_count, latent_width
        )
        flat_rope = rope_query[request * stretch_rows : (request + 1) * stretch_rows].reshape(
            stretch_rows * head_count, rope_width
        )
        scores = jnp.einsum(
            "ql,pl->qp", flat_latent, cache_latent[request], preferred_element_type=jnp.float32
        )
        scores = (
            scores + jnp.dot(flat_rope, cache_rope[request], preferred_element_type=jnp.float32)
        ) * softmax_scale
        last_seen = (
            cached_length[request]
            + jnp.arange(stretch_rows * head_count, dtype=jnp.int32) // head_count
        )
        visible = positions[None, :] <= last_seen[:, None]
        scores = jnp.where(visible, scores, masked_score)
        block_peak = jnp.max(scores, axis=1)
        weights = jnp.where(visible, jnp.exp(scores - block_peak[:, None]), 0.0)
        block_sum = jnp.sum(weights, axis=1)
        block_pool = jnp.dot(
            weights.astype(jnp.bfloat16), cache_latent[request], preferred_element_type=jnp.float32
        )
        peak_list.append(block_peak.reshape(stretch_rows, head_count))
        sum_list.append(block_sum.reshape(stretch_rows, head_count))
        pool_list.append(block_pool.reshape(stretch_rows, head_count, latent_width))
    return (
        jnp.concatenate(peak_list, axis=0),
        jnp.concatenate(sum_list, axis=0),
        jnp.concatenate(pool_list, axis=0),
    )


def project_heads(pooled, weight_sum, value_up, out_weight):
    attended = (pooled / weight_sum[:, :, None]).astype(jnp.bfloat16)
    head_values = jnp.einsum(
        "rhl,hlv->rhv", attended, value_up, preferred_element_type=jnp.float32
    ).astype(jnp.bfloat16)
    return jnp.dot(
        head_values.reshape(head_values.shape[0], -1),
        out_weight,
        preferred_element_type=jnp.float32,
    )


def local(
    query_input,
    query_gain,
    nope_weight,
    rope_weight,
    key_up,
    value_up,
    out_weight,
    cache_latent,
    cache_rope,
    cached_length,
):
    head_local = key_up.shape[0]
    nope_width = key_up.shape[1]
    rope_width = rope_weight.shape[1] // head_local
    row_count = query_input.shape[0]
    key_count = cache_latent.shape[1]
    widened = query_input.astype(jnp.float32)
    normed = (
        widened
        * lax.rsqrt(jnp.mean(widened * widened, axis=-1, keepdims=True) + 1e-06)
        * query_gain.astype(jnp.float32)
    ).astype(jnp.bfloat16)
    query_nope = (
        jnp.dot(normed, nope_weight, preferred_element_type=jnp.float32)
        .astype(jnp.bfloat16)
        .reshape(row_count, head_local, nope_width)
    )
    query_rope = (
        jnp.dot(normed, rope_weight, preferred_element_type=jnp.float32)
        .astype(jnp.bfloat16)
        .reshape(row_count, head_local, rope_width)
    )
    query_latent = jnp.einsum(
        "rhn,hnl->rhl", query_nope, key_up, preferred_element_type=jnp.float32
    ).astype(jnp.bfloat16)
    softmax_scale = mscale_yarn * mscale_yarn / math.sqrt(nope_width + rope_width)
    positions = lax.axis_index("ctx") * key_count + jnp.arange(key_count, dtype=jnp.int32)
    every_latent, every_rope = (
        lax.all_gather(query_latent, "ctx", axis=1, tiled=True),
        lax.all_gather(query_rope, "ctx", axis=1, tiled=True),
    )
    block_peak, block_sum, block_pool = attend_heads(
        every_latent, every_rope, cache_latent, cache_rope, cached_length, positions, softmax_scale
    )
    pooled_in = lax.all_to_all(block_pool[None], "ctx", split_axis=2, concat_axis=0, tiled=True)
    peak_in = lax.all_to_all(block_peak[None], "ctx", split_axis=2, concat_axis=0, tiled=True)
    sum_in = lax.all_to_all(block_sum[None], "ctx", split_axis=2, concat_axis=0, tiled=True)
    row_top = jnp.max(peak_in, axis=0)
    factor = jnp.exp(peak_in - row_top[None])
    pooled = jnp.sum(pooled_in * factor[..., None], axis=0)
    weight_sum = jnp.sum(sum_in * factor, axis=0)
    partial_value = project_heads(pooled, weight_sum, value_up, out_weight)
    return lax.psum(partial_value, "ctx").astype(jnp.bfloat16)


def solution(mesh):
    placed = (
        P("groups", None),
        P(),
        P(None, "ctx"),
        P(None, "ctx"),
        P("ctx", None, None),
        P("ctx", None, None),
        P("ctx", None),
        P("groups", "ctx", None),
        P("groups", None, "ctx"),
        P("groups"),
    )
    return jax.shard_map(
        local, mesh=mesh, in_specs=placed, out_specs=P("groups", None), check_vma=False
    )
```

profile of v0, /device:TPU:0, one launch (start us, length us, event | category | flops | bytes accessed | tf_op | source)
XLA Modules:
  0.0 175.1 jit_solution(12115778293265833145)
XLA Ops:
  0.0 0.0 copy-start
  0.0 0.0 copy-start.4
  0.0 0.0 copy-start.5
  0.0 1.4 fusion.44
  1.4 0.7 convert_element_type.40
  2.1 0.9 fusion.28
  3.1 0.0 copy-done
  3.1 1.1 fusion.21
  4.1 1.1 fusion.20
  5.2 24.6 %all_gather.6 = bf16[16,32,512]{2,0,1:T(8,128)(2,1)S(1)} all-gather(bf16[16,2,512]{2,0,1:T(8,128)(2,1)S(1)} %fusion.20), channel_id=1, replica_groups=mesh['groups'=2,'ctx'=16] {'ctx'}, dimensions={1}, use_global_device_ids=true | all-gather | bytes 557056 | tf_op jit(solution)/shard_map/all_gather | solution.py:105
  29.9 0.1 copy.76
  30.0 0.0 copy-done.4
  30.0 0.0 copy-done.5
  30.0 0.2 convolution_convert_fusion.3
  30.2 0.1 reshape.79
  30.3 17.8 %all_gather.7 = bf16[16,32,64]{2,0,1:T(8,128)(2,1)S(1)} all-gather(bf16[16,2,64]{2,0,1:T(8,128)(2,1)S(1)} %copy.64), channel_id=1, replica_groups=mesh['groups'=2,'ctx'=16] {'ctx'}, dimensions={1}, use_global_device_ids=true | all-gather | bytes 69632 | tf_op jit(solution)/shard_map/all_gather | solution.py:106
  48.1 0.1 copy.75
  48.2 0.0 copy-start.1
  48.2 2.5 %fusion.6 = f32[256,2048]{1,0:T(8,128)S(1)} fusion(bf16[256,512]{1,0:T(8,128)(2,1)S(1)} %bitcast.80, bf16[2,2048,512]{2,1,0:T(8,128)(2,1)} %param.17), kind=kOutput, calls=%fused_computation.10 | convolution fusion | flops 536870912 | bytes 4456448 | tf_op jit(solution)/shard_map/ql,pl->qp/dot_general | solution.py:26
  50.7 0.3 copy-done.1
  51.0 0.0 copy-start.3
  51.0 0.7 fusion.10
  51.8 1.3 broadcast_add_fusion
  53.1 0.0 copy-done.3
  53.1 0.6 fusion.46
  53.8 0.6 fusion.45
  54.4 1.0 fusion.16
  55.5 0.1 reshape.85
  55.5 0.1 reshape.86
  55.6 0.7 copy.72
  56.3 3.5 %all-to-all-start.2 = ((f32[1,16,32]{1,0,2:T(1,128)}), f32[1,16,32]{1,0,2:T(1,128)S(1)}, u32[]{:S(2)}, u32[]{:S(2)}) async-start(f32[1,16,32]{1,0,2:T(1,128)} %copy.72), calls=%async_computation.2 | async-start | bytes 32768 | tf_op jit(solution)/shard_map/all_to_all | solution.py:113
  59.8 0.1 reshape.84
  59.9 0.1 reshape.83
  60.0 0.0 copy-start.2
  60.0 2.4 %fusion.4 = f32[8,32,512]{2,1,0:T(8,128)S(1)} fusion(bf16[8,32,2048]{2,1,0:T(8,128)(2,1)S(1)} %bitcast.79, bf16[2,2048,512]{2,1,0:T(8,128)(2,1)} %param.17), kind=kOutput, calls=%fused_computation.8 | convolution fusion | flops 536870912 | bytes 3670016 | tf_op jit(solution)/shard_map/dot_general | solution.py:41
  62.4 0.4 copy-done.2
  62.8 0.7 fusion.8
  63.5 0.7 copy.70
  64.2 2.1 %all-to-all-done.2 = f32[1,16,32]{1,0,2:T(1,128)S(1)} async-done(((f32[1,16,32]{1,0,2:T(1,128)}), f32[1,16,32]{1,0,2:T(1,128)S(1)}, u32[]{:S(2)}, u32[]{:S(2)}) %all-to-all-start.2) | async-done | bytes 2080 | tf_op jit(solution)/shard_map/all_to_all | solution.py:113
  66.3 3.9 %all-to-all-start.1 = ((f32[1,16,32]{1,0,2:T(1,128)}), f32[1,16,32]{1,0,2:T(1,128)S(1)}, u32[]{:S(2)}, u32[]{:S(2)}) async-start(f32[1,16,32]{1,0,2:T(1,128)} %copy.70), calls=%async_computation.1 | async-start | bytes 32768 | tf_op jit(solution)/shard_map/all_to_all | solution.py:112
  70.2 0.1 maximum_bitcast_fusion
  70.3 1.6 copy.68
  71.9 0.0 copy-start.6
  71.9 4.8 %all-to-all-done.1 = f32[1,16,32]{1,0,2:T(1,128)S(1)} async-done(((f32[1,16,32]{1,0,2:T(1,128)}), f32[1,16,32]{1,0,2:T(1,128)S(1)}, u32[]{:S(2)}, u32[]{:S(2)}) %all-to-all-start.1) | async-done | bytes 2080 | tf_op jit(solution)/shard_map/all_to_all | solution.py:112
  76.7 3.7 %all-to-all-start = ((f32[1,16,32,512]{3,1,0,2:T(8,128)}), f32[1,16,32,512]{3,1,0,2:T(8,128)S(1)}, u32[]{:S(2)}, u32[]{:S(2)}) async-start(f32[1,16,32,512]{3,1,0,2:T(8,128)} %copy.68), calls=%async_computation | async-start | bytes 2097152 | tf_op jit(solution)/shard_map/all_to_all | solution.py:111
  80.4 0.2 copy.71
  80.6 22.6 %all-to-all-done = f32[1,16,32,512]{3,1,0,2:T(8,128)S(1)} async-done(((f32[1,16,32,512]{3,1,0,2:T(8,128)}), f32[1,16,32,512]{3,1,0,2:T(8,128)S(1)}, u32[]{:S(2)}, u32[]{:S(2)}) %all-to-all-start) | async-done | bytes 1048608 | tf_op jit(solution)/shard_map/all_to_all | solution.py:111
  103.2 1.1 fusion.23
  104.3 0.0 copy-done.6
  104.3 0.2 fusion.22
  104.5 2.6 %fusion.36 = f32[16,7168]{1,0:T(8,128)S(1)} fusion(bf16[256,7168]{1,0:T(8,128)(2,1)} %param.16, bf16[2,2,8,128]{3,2,1,0:T(8,128)(2,1)S(1)} %fusion.22), kind=kOutput, calls=%fused_computation.48 | convolution fusion | flops 58720256 | bytes 4136960 | tf_op jit(solution)/shard_map/dot_general | solution.py:59
  107.1 68.0 %all-reduce.1 = bf16[16,7168]{1,0:T(8,128)(2,1)} all-reduce(f32[16,7168]{1,0:T(8,128)S(1)} %fusion.36), channel_id=1, replica_groups=mesh['groups'=2,'ctx'=16] {'ctx'}, use_global_device_ids=true, to_apply=%region_8.9 | all-reduce | flops 114688 | bytes 688128 | tf_op jit(solution)/shard_map/psum | solution.py:119
  (11 shorter events, 0.2 us)
Async XLA Ops:
  0.0 3.1 %copy-start = (bf16[1536,256]{1,0:T(8,128)(2,1)S(1)}, bf16[1536,256]{1,0:T(8,128)(2,1)}, u32[]{:S(2)}) copy-start(bf16[1536,256]{1,0:T(8,128)(2,1)} %param.12) | copy-start | bytes 2359300
  0.0 30.0 %copy-start.4 = (bf16[16,1536]{1,0:T(8,128)(2,1)S(1)}, bf16[16,1536]{1,0:T(8,128)(2,1)}, u32[]{:S(2)}) copy-start(bf16[16,1536]{1,0:T(8,128)(2,1)} %param.10) | copy-start | bytes 147460
  0.0 30.0 %copy-start.5 = (bf16[1536,128]{1,0:T(8,128)(2,1)S(1)}, bf16[1536,128]{1,0:T(8,128)(2,1)}, u32[]{:S(2)}) copy-start(bf16[1536,128]{1,0:T(8,128)(2,1)} %param.13) | copy-start | bytes 1179652
  48.2 2.8 %copy-start.1 = (bf16[2,2048,512]{2,1,0:T(8,128)(2,1)S(1)}, bf16[2,2048,512]{2,1,0:T(8,128)(2,1)}, u32[]{:S(2)}) copy-start(bf16[2,2048,512]{2,1,0:T(8,128)(2,1)} %param.17) | copy-start | bytes 12582916
  51.0 2.1 %copy-start.3 = (bf16[2,64,2048]{2,1,0:T(8,128)(2,1)S(1)}, bf16[2,64,2048]{2,1,0:T(8,128)(2,1)}, u32[]{:S(2)}) copy-start(bf16[2,64,2048]{2,1,0:T(8,128)(2,1)} %param.18) | copy-start | bytes 1572868
  56.3 10.0 %all-to-all-start.2 = ((f32[1,16,32]{1,0,2:T(1,128)}), f32[1,16,32]{1,0,2:T(1,128)S(1)}, u32[]{:S(2)}, u32[]{:S(2)}) async-start(f32[1,16,32]{1,0,2:T(1,128)} %copy.72), calls=%async_computation.2 | async-start | bytes 32768 | tf_op jit(solution)/shard_map/all_to_all | solution.py:113
  60.0 2.8 %copy-start.2 = (bf16[2,2048,512]{2,1,0:T(8,128)(2,1)S(1)}, bf16[2,2048,512]{2,1,0:T(8,128)(2,1)}, u32[]{:S(2)}) copy-start(bf16[2,2048,512]{2,1,0:T(8,128)(2,1)} %param.17) | copy-start | bytes 12582916
  66.3 10.4 %all-to-all-start.1 = ((f32[1,16,32]{1,0,2:T(1,128)}), f32[1,16,32]{1,0,2:T(1,128)S(1)}, u32[]{:S(2)}, u32[]{:S(2)}) async-start(f32[1,16,32]{1,0,2:T(1,128)} %copy.70), calls=%async_computation.1 | async-start | bytes 32768 | tf_op jit(solution)/shard_map/all_to_all | solution.py:112
  71.9 32.4 %copy-start.6 = (bf16[2,512,128]{2,1,0:T(8,128)(2,1)S(1)}, bf16[2,512,128]{2,1,0:T(8,128)(2,1)}, u32[]{:S(2)}) copy-start(bf16[2,512,128]{2,1,0:T(8,128)(2,1)} %param.15) | copy-start | bytes 786436
  76.7 26.5 %all-to-all-start = ((f32[1,16,32,512]{3,1,0,2:T(8,128)}), f32[1,16,32,512]{3,1,0,2:T(8,128)S(1)}, u32[]{:S(2)}, u32[]{:S(2)}) async-start(f32[1,16,32,512]{3,1,0,2:T(8,128)} %copy.68), calls=%async_computation | async-start | bytes 2097152 | tf_op jit(solution)/shard_map/all_to_all | solution.py:111
where the time goes:
time: 176 us; the launch traced here: 175 us
  blocking collectives  110 us (62%)
  waiting for transfers between devices  29.5 us (17%)
  matrix products  12.8 us (7%)
  starting transfers between devices  11 us (6%)
  local copies, waits for them, and re-layouts  5.92 us (3%)
  other arithmetic  5.27 us (3%)
    psum x1, blocking collectives, local(): return lax.psum(partial_value, 'ctx').astype(jnp.bfloat16)  68 us
    all_gather x1, blocking collectives, local(): lax.all_gather(query_latent, 'ctx', axis=1, tiled=True)  24.6 us
    all_to_all x1, waiting for transfers between devices, local(): lax.all_to_all(block_pool[None], 'ctx', split_axis=2, concat_axis=0, tile...  22.6 us
    all_gather x1, blocking collectives, local(): lax.all_gather(query_rope, 'ctx', axis=1, tiled=True)  17.8 us
    all_to_all x1, waiting for transfers between devices, local(): lax.all_to_all(block_peak[None], 'ctx', split_axis=2, concat_axis=0, tile...  4.8 us
    all_to_all x1, starting transfers between devices, local(): lax.all_to_all(block_peak[None], 'ctx', split_axis=2, concat_axis=0, tile...  3.88 us
    all_to_all x1, starting transfers between devices, local(): lax.all_to_all(block_pool[None], 'ctx', split_axis=2, concat_axis=0, tile...  3.65 us
  transfers between devices with their start and end apart: 3, of which 3 were waited for; matrix products, arithmetic and copies ran while one was open for 3% of the time, Pallas kernels for 0%

commit v1 on v0

--- a/solution.py
+++ b/solution.py
@@ -108,7 +108,12 @@
     block_peak, block_sum, block_pool = attend_heads(
         every_latent, every_rope, cache_latent, cache_rope, cached_length, positions, softmax_scale
     )
-    pooled_in = lax.all_to_all(block_pool[None], "ctx", split_axis=2, concat_axis=0, tiled=True)
+    pooled_in = jnp.concatenate(
+        lax.all_to_all(
+            jnp.stack(jnp.split(block_pool[None], lax.axis_size("ctx"), axis=2)), "ctx", 0, 0
+        ),
+        axis=0,
+    )
     peak_in = lax.all_to_all(block_peak[None], "ctx", split_axis=2, concat_axis=0, tiled=True)
     sum_in = lax.all_to_all(block_sum[None], "ctx", split_axis=2, concat_axis=0, tiled=True)
     row_top = jnp.max(peak_in, axis=0)

time: 176 us -> 185 us (1.051)
  local copies, waits for them, and re-layouts: 5.92 us -> 14.6 us
  starting transfers between devices: 11 us -> 13.1 us
    unnamed x16 -> x31, local copies, waits for them, and re-layouts: 0.88 us -> 10.6 us
    all_to_all x1, waiting for transfers between devices: 2.1 us -> 0.01 us  [local(): lax.all_to_all(block_sum[None], 'ctx', split_axis=2, concat_axis=0, tiled...]
    all_to_all x1, starting transfers between devices: 3.88 us -> 5.97 us  [local(): lax.all_to_all(block_peak[None], 'ctx', split_axis=2, concat_axis=0, tile...]
  transfers between devices with their start and end apart: 3 -> 3, of which waited for: 3 -> 2; matrix products, arithmetic and copies ran while one was open for 3% -> 8% of each run, Pallas kernels for 0% -> 0%
where the time goes in v1:
time: 185 us; the launch traced here: 184 us
  blocking collectives  110 us (59%)
  waiting for transfers between devices  28.5 us (15%)
  local copies, waits for them, and re-layouts  14.6 us (8%)
  starting transfers between devices  13.1 us (7%)
  matrix products  12.8 us (7%)
  other arithmetic  4.66 us (3%)
    psum x1, blocking collectives, local(): return lax.psum(partial_value, 'ctx').astype(jnp.bfloat16)  68 us
    all_gather x1, blocking collectives, local(): lax.all_gather(query_latent, 'ctx', axis=1, tiled=True)  24.6 us
    all_to_all x1, waiting for transfers between devices, local(): lax.all_to_all(jnp.stack(jnp.split(block_pool[None], lax.axis_size('ctx')...  22.6 us
    all_gather x1, blocking collectives, local(): lax.all_gather(query_rope, 'ctx', axis=1, tiled=True)  17.8 us
    unnamed x31, local copies, waits for them, and re-layouts  10.6 us
    all_to_all x1, starting transfers between devices, local(): lax.all_to_all(block_peak[None], 'ctx', split_axis=2, concat_axis=0, tile...  5.97 us
    all_to_all x1, waiting for transfers between devices, local(): lax.all_to_all(block_peak[None], 'ctx', split_axis=2, concat_axis=0, tile...  5.84 us
  transfers between devices with their start and end apart: 3, of which 2 were waited for; matrix products, arithmetic and copies ran while one was open for 8% of the time, Pallas kernels for 0%

profile of v1, /device:TPU:0, one launch (start us, length us, event | category | flops | bytes accessed | tf_op | source)
XLA Modules:
  0.0 184.3 jit_solution(543909023371158633)
XLA Ops:
  0.0 0.0 copy-start
  0.0 0.0 copy-start.4
  0.0 0.0 copy-start.5
  0.0 1.4 fusion.60
  1.4 0.7 convert_element_type.40
  2.1 0.9 fusion.28
  3.1 0.0 copy-done
  3.1 1.1 fusion.21
  4.1 1.1 fusion.20
  5.2 24.6 %all_gather.6 = bf16[16,32,512]{2,0,1:T(8,128)(2,1)S(1)} all-gather(bf16[16,2,512]{2,0,1:T(8,128)(2,1)S(1)} %fusion.20), channel_id=1, replica_groups=mesh['groups'=2,'ctx'=16] {'ctx'}, dimensions={1}, use_global_device_ids=true | all-gather | bytes 557056 | tf_op jit(solution)/shard_map/all_gather | solution.py:105
  29.9 0.1 copy.68
  30.0 0.0 copy-done.4
  30.0 0.0 copy-done.5
  30.0 0.2 convolution_convert_fusion.3
  30.2 0.1 reshape.82
  30.3 17.8 %all_gather.7 = bf16[16,32,64]{2,0,1:T(8,128)(2,1)S(1)} all-gather(bf16[16,2,64]{2,0,1:T(8,128)(2,1)S(1)} %copy.58), channel_id=1, replica_groups=mesh['groups'=2,'ctx'=16] {'ctx'}, dimensions={1}, use_global_device_ids=true | all-gather | bytes 69632 | tf_op jit(solution)/shard_map/all_gather | solution.py:106
  48.1 0.1 copy.67
  48.2 0.0 copy-start.1
  48.2 2.5 %fusion.6 = f32[256,2048]{1,0:T(8,128)S(1)} fusion(bf16[256,512]{1,0:T(8,128)(2,1)S(1)} %bitcast.140, bf16[2,2048,512]{2,1,0:T(8,128)(2,1)} %param.17), kind=kOutput, calls=%fused_computation.10 | convolution fusion | flops 536870912 | bytes 4456448 | tf_op jit(solution)/shard_map/ql,pl->qp/dot_general | solution.py:26
  50.7 0.3 copy-done.1
  51.0 0.7 fusion.10
  51.8 1.3 broadcast_add_fusion
  53.1 0.0 copy-done.3
  53.1 0.6 fusion.62
  53.8 0.6 fusion.61
  54.4 1.0 fusion.16
  55.5 0.1 reshape.89
  55.5 0.1 reshape.90
  55.6 0.7 copy.64
  56.3 3.5 %all-to-all-start.2 = ((f32[1,16,32]{1,0,2:T(1,128)}), f32[1,16,32]{1,0,2:T(1,128)S(1)}, u32[]{:S(2)}, u32[]{:S(2)}) async-start(f32[1,16,32]{1,0,2:T(1,128)} %copy.64), calls=%async_computation.2 | async-start | bytes 32768 | tf_op jit(solution)/shard_map/all_to_all | solution.py:118
  59.8 0.1 reshape.88
  59.9 0.1 reshape.87
  60.0 2.4 %fusion.4 = f32[8,32,512]{2,1,0:T(8,128)S(1)} fusion(bf16[8,32,2048]{2,1,0:T(8,128)(2,1)S(1)} %bitcast.139, bf16[2,2048,512]{2,1,0:T(8,128)(2,1)} %param.17), kind=kOutput, calls=%fused_computation.8 | convolution fusion | flops 536870912 | bytes 3670016 | tf_op jit(solution)/shard_map/dot_general | solution.py:41
  62.4 0.4 copy-done.2
  62.8 0.7 fusion.8
  63.5 0.1 maximum_bitcast_fusion
  63.6 0.6 fusion.46
  64.2 0.6 fusion.45
  64.9 0.6 fusion.44
  65.5 0.6 fusion.43
  66.2 0.6 fusion.42
  66.8 0.7 fusion.41
  67.5 0.6 fusion.40
  68.1 0.6 fusion.39
  68.8 0.6 fusion.38
  69.4 0.6 fusion.37
  70.1 0.6 fusion.36
  70.7 0.6 fusion.35
  71.3 0.6 fusion.34
  72.0 0.6 fusion.33
  72.6 0.7 fusion.32
  73.3 0.7 copy.62
  74.0 0.0 all-to-all-done.2
  74.0 6.0 %all-to-all-start.1 = ((f32[1,16,32]{1,0,2:T(1,128)}), f32[1,16,32]{1,0,2:T(1,128)S(1)}, u32[]{:S(2)}, u32[]{:S(2)}) async-start(f32[1,16,32]{1,0,2:T(1,128)} %copy.62), calls=%async_computation.1 | async-start | bytes 32768 | tf_op jit(solution)/shard_map/all_to_all | solution.py:117
  79.9 0.7 fusion.31
  80.6 5.8 %all-to-all-done.1 = f32[1,16,32]{1,0,2:T(1,128)S(1)} async-done(((f32[1,16,32]{1,0,2:T(1,128)}), f32[1,16,32]{1,0,2:T(1,128)S(1)}, u32[]{:S(2)}, u32[]{:S(2)}) %all-to-all-start.1) | async-done | bytes 2080 | tf_op jit(solution)/shard_map/all_to_all | solution.py:117
  86.4 3.7 %all-to-all-start = ((f32[16,1,16,2,512]{4,3,2,1,0:T(2,128)}), f32[16,1,16,2,512]{4,3,2,1,0:T(2,128)S(1)}, u32[]{:S(2)}, u32[]{:S(2)}) async-start(f32[16,1,16,2,512]{4,3,2,1,0:T(2,128)} %fusion.31), calls=%async_computation | async-start | bytes 2097152 | tf_op jit(solution)/shard_map/all_to_all | solution.py:112
  90.2 0.2 copy.63
  90.3 22.6 %all-to-all-done = f32[16,1,16,2,512]{4,3,2,1,0:T(2,128)S(1)} async-done(((f32[16,1,16,2,512]{4,3,2,1,0:T(2,128)}), f32[16,1,16,2,512]{4,3,2,1,0:T(2,128)S(1)}, u32[]{:S(2)}, u32[]{:S(2)}) %all-to-all-start) | async-done | bytes 1048608 | tf_op jit(solution)/shard_map/all_to_all | solution.py:112
  113.0 0.5 fusion.23
  113.5 0.0 copy-done.6
  113.5 0.2 fusion.22
  113.7 2.6 %fusion.52 = f32[16,7168]{1,0:T(8,128)S(1)} fusion(bf16[256,7168]{1,0:T(8,128)(2,1)} %param.16, bf16[2,2,8,128]{3,2,1,0:T(8,128)(2,1)S(1)} %fusion.22), kind=kOutput, calls=%fused_computation.80 | convolution fusion | flops 58720256 | bytes 4136960 | tf_op jit(solution)/shard_map/dot_general | solution.py:59
  116.3 68.0 %all-reduce.1 = bf16[16,7168]{1,0:T(8,128)(2,1)} all-reduce(f32[16,7168]{1,0:T(8,128)S(1)} %fusion.52), channel_id=1, replica_groups=mesh['groups'=2,'ctx'=16] {'ctx'}, use_global_device_ids=true, to_apply=%region_8.9 | all-reduce | flops 114688 | bytes 688128 | tf_op jit(solution)/shard_map/psum | solution.py:124
  (14 shorter events, 0.2 us)
Async XLA Ops:
  0.0 3.1 %copy-start = (bf16[1536,256]{1,0:T(8,128)(2,1)S(1)}, bf16[1536,256]{1,0:T(8,128)(2,1)}, u32[]{:S(2)}) copy-start(bf16[1536,256]{1,0:T(8,128)(2,1)} %param.12) | copy-start | bytes 2359300
  0.0 30.0 %copy-start.4 = (bf16[16,1536]{1,0:T(8,128)(2,1)S(1)}, bf16[16,1536]{1,0:T(8,128)(2,1)}, u32[]{:S(2)}) copy-start(bf16[16,1536]{1,0:T(8,128)(2,1)} %param.10) | copy-start | bytes 147460
  0.0 30.0 %copy-start.5 = (bf16[1536,128]{1,0:T(8,128)(2,1)S(1)}, bf16[1536,128]{1,0:T(8,128)(2,1)}, u32[]{:S(2)}) copy-start(bf16[1536,128]{1,0:T(8,128)(2,1)} %param.13) | copy-start | bytes 1179652
  48.2 2.8 %copy-start.1 = (bf16[2,2048,512]{2,1,0:T(8,128)(2,1)S(1)}, bf16[2,2048,512]{2,1,0:T(8,128)(2,1)}, u32[]{:S(2)}) copy-start(bf16[2,2048,512]{2,1,0:T(8,128)(2,1)} %param.17) | copy-start | bytes 12582916
  51.0 2.1 %copy-start.3 = (bf16[2,64,2048]{2,1,0:T(8,128)(2,1)S(1)}, bf16[2,64,2048]{2,1,0:T(8,128)(2,1)}, u32[]{:S(2)}) copy-start(bf16[2,64,2048]{2,1,0:T(8,128)(2,1)} %param.18) | copy-start | bytes 1572868
  56.3 17.6 %all-to-all-start.2 = ((f32[1,16,32]{1,0,2:T(1,128)}), f32[1,16,32]{1,0,2:T(1,128)S(1)}, u32[]{:S(2)}, u32[]{:S(2)}) async-start(f32[1,16,32]{1,0,2:T(1,128)} %copy.64), calls=%async_computation.2 | async-start | bytes 32768 | tf_op jit(solution)/shard_map/all_to_all | solution.py:118
  60.0 2.8 %copy-start.2 = (bf16[2,2048,512]{2,1,0:T(8,128)(2,1)S(1)}, bf16[2,2048,512]{2,1,0:T(8,128)(2,1)}, u32[]{:S(2)}) copy-start(bf16[2,2048,512]{2,1,0:T(8,128)(2,1)} %param.17) | copy-start | bytes 12582916
  71.3 42.1 %copy-start.6 = (bf16[2,512,128]{2,1,0:T(8,128)(2,1)S(1)}, bf16[2,512,128]{2,1,0:T(8,128)(2,1)}, u32[]{:S(2)}) copy-start(bf16[2,512,128]{2,1,0:T(8,128)(2,1)} %param.15) | copy-start | bytes 786436
  74.0 12.5 %all-to-all-start.1 = ((f32[1,16,32]{1,0,2:T(1,128)}), f32[1,16,32]{1,0,2:T(1,128)S(1)}, u32[]{:S(2)}, u32[]{:S(2)}) async-start(f32[1,16,32]{1,0,2:T(1,128)} %copy.62), calls=%async_computation.1 | async-start | bytes 32768 | tf_op jit(solution)/shard_map/all_to_all | solution.py:117
  86.4 26.5 %all-to-all-start = ((f32[16,1,16,2,512]{4,3,2,1,0:T(2,128)}), f32[16,1,16,2,512]{4,3,2,1,0:T(2,128)S(1)}, u32[]{:S(2)}, u32[]{:S(2)}) async-start(f32[16,1,16,2,512]{4,3,2,1,0:T(2,128)} %fusion.31), calls=%async_computation | async-start | bytes 2097152 | tf_op jit(solution)/shard_map/all_to_all | solution.py:112
